TPU v7x, 512 devices: a whole 4x4x16 slice. The times are simulated.
512 devices in a mesh: ktot: 32 (over z_lo, y, core), kvir: 16 (over z_hi, x).
Axes of the slice: x: 4, y: 4, z: 16 (z_hi: 4, z_lo: 4; z = z_hi * 4 + z_lo), core: 2. Of those that a mesh axis runs over, the one named last changes fastest.
Arguments:
- amplitudes: bfloat16 [32, 16, 672, 1024], P('ktot', 'kvir'), may hold values from -6 to 6
- ladder_integrals: bfloat16 [32, 16, 1024, 1024], P('ktot', 'kvir'), may hold values from -0.046875 to 0.046875
- listed: int32 [32, 16], P('ktot', 'kvir'), may hold values 0 or 1
- current: bfloat16 [32, 672, 1024], P('ktot', 'kvir'), may hold values from -3 to 3
- denominators: float32 [32, 672, 1024], P('ktot', 'kvir'), may hold values from 2 to 8
- cycle_integrals: bfloat16 [32, 512, 512], P('ktot', 'kvir'), may hold values from -0.25 to 0.25
Outputs:
- ladder_res: bfloat16 [32, 672, 1024], P('ktot', 'kvir')
- cycle_res: float32 [32, 1344, 1344], P('ktot', 'kvir')
All inputs are finite; a program needn't handle non-finite values. No bound on the sum of `listed` on one device may be relied on, other than what follows from the above.
Results may differ from a plain program's by a relative error of at most 0.017.
Values may be sent and summed in bfloat16 or wider, within the bound.
No kernel may reach another device: no remote copies, remote signals or barrier semaphores. Data moves between devices by JAX's collectives and lax.ppermute only.
A program may use at most 64 MiB of HBM per device.

v0:
```python
import jax
import jax.numpy as jnp
from jax import lax
from jax.sharding import PartitionSpec as P


def shards(amplitudes, ladder_integrals, listed, current, denominators, cycle_integrals):
    amp_block = amplitudes[0, 0]
    weights = ladder_integrals[0, 0]
    scale_mask = listed[0, 0].astype(jnp.float32)
    rows_dev = current.shape[1]
    width = current.shape[2]
    tot_count = lax.axis_size("ktot")
    vir_count = lax.axis_size("kvir")
    summed = lax.psum(
        jnp.dot(amp_block, weights, preferred_element_type=jnp.float32) * scale_mask, "kvir"
    )
    ladder = lax.dynamic_slice_in_dim(summed, lax.axis_index("kvir") * rows_dev, rows_dev, 0)
    updated = (current[0].astype(jnp.float32) + ladder / denominators[0]).astype(jnp.bfloat16)
    col_width = width // tot_count
    received = lax.all_to_all(
        updated.reshape(rows_dev, tot_count, col_width),
        "ktot",
        split_axis=1,
        concat_axis=1,
        tiled=True,
    )
    local_cycle = received.reshape(rows_dev * tot_count, col_width)
    cycle_rows = local_cycle.shape[0]
    cycle_weights = cycle_integrals[0]
    cycle_width = cycle_weights.shape[1]
    share_rows = cycle_rows // vir_count
    my_start = lax.axis_index("kvir") * share_rows
    partial_cycle = jnp.dot(local_cycle, cycle_weights, preferred_element_type=jnp.float32)
    partial_cycle = partial_cycle.astype(jnp.bfloat16).astype(jnp.float32)
    summed_cycle = lax.psum(partial_cycle.astype(jnp.bfloat16), "kvir").astype(jnp.float32)
    cycle_mixed = lax.dynamic_slice_in_dim(summed_cycle, my_start, share_rows, 0).astype(
        jnp.bfloat16
    )
    cycle_out = lax.dot_general(
        cycle_mixed,
        lax.all_gather(local_cycle, "kvir", axis=1, tiled=True),
        (((1,), (1,)), ((), ())),
        preferred_element_type=jnp.float32,
    )
    return (ladder.astype(jnp.bfloat16)[None], (cycle_out * cycle_width ** (-0.5))[None])


def solution(mesh):
    return jax.shard_map(
        shards,
        mesh=mesh,
        in_specs=(
            P("ktot", "kvir", None, None),
            P("ktot", "kvir", None, None),
            P("ktot", "kvir"),
            P("ktot", "kvir", None),
            P("ktot", "kvir", None),
            P("ktot", "kvir", None),
        ),
        out_specs=(P("ktot", "kvir", None), P("ktot", "kvir", None)),
        check_vma=False,
    )
```

profile of v0, /device:TPU:8, one launch (start us, length us, event | category | flops | bytes accessed | tf_op | source)
XLA Modules:
  0.0 652.3 jit_solution(10469983389552584151)
XLA Ops:
  7.2 0.0 copy-start
  7.2 0.0 all-reduce.3.cloned.1.call-start
  8.0 0.8 copy-done
  8.8 4.5 fusion.3
  13.3 0.0 all-reduce.3.cloned.1.call-update
  13.3 0.0 all-reduce.5.cloned.1.call-start
  13.4 298.0 %all-reduce.3.cloned.1.call-done = f32[672,1024]{1,0:T(8,128)} async-done(((f32[672,1024]{1,0:T(8,128)}), f32[672,1024]{1,0:T(8,128)}) %all-reduce.3.cloned.1.call-update) | async-done | bytes 2752528 | tf_op jit(solution)/shard_map/psum | solution.py:15
  311.4 1.0 fusion.8
  312.4 0.2 copy.15
  312.6 0.4 reshape.16
  312.9 18.6 %all_to_all.5 = bf16[32,2,672]{2,1,0:T(2,128)(2,1)S(1)} all-to-all(bf16[32,2,672]{2,1,0:T(2,128)(2,1)S(1)} %reshape.16), channel_id=1, replica_groups=mesh['ktot'=32,'kvir'=16] {'ktot'}, dimensions={0} | all-to-all | bytes 172032 | tf_op jit(solution)/shard_map/all_to_all | solution.py:21
  331.6 0.4 reshape.17
  332.0 0.4 copy.13
  332.4 0.3 reshape.14
  332.7 0.0 copy-start.1
  332.7 1.6 convolution_convert_fusion
  334.4 0.0 all-reduce.5.cloned.1.call-update
  334.4 0.0 all-gather.2.cloned.1.call-start
  334.5 0.7 all-gather.2.cloned.1.call-update
  335.1 1.6 fusion.9
  336.7 219.6 %all-reduce.5.cloned.1.call-done = bf16[1344,512]{1,0:T(8,128)(2,1)} async-done(((bf16[1344,512]{1,0:T(8,128)(2,1)}), bf16[1344,512]{1,0:T(8,128)(2,1)}) %all-reduce.5.cloned.1.call-update) | async-done | bytes 1376272 | tf_op jit(solution)/shard_map/psum | solution.py:36
  556.3 86.4 %all-gather.2.cloned.1.call-done = bf16[1344,512]{0,1:T(8,128)(2,1)} async-done(((bf16[1344,32]{0,1:T(8,128)(2,1)}), bf16[1344,512]{0,1:T(8,128)(2,1)}) %all-gather.2.cloned.1.call-update) | async-done | bytes 1376272 | tf_op jit(solution)/shard_map/all_gather | solution.py:42
  642.7 1.8 fusion
  644.5 1.3 copy.14
  (7 shorter events, 0.0 us)
Async XLA Ops:
  7.2 1.6 copy-start
  7.2 304.2 %all-reduce.3.cloned.1.call-start = ((), (), s32[]{:S(2)}) async-start(), calls=%async_computation.1 | async-start | bytes 5505024 | tf_op jit(solution)/shard_map/psum | solution.py:15
  13.3 298.1 %copy-start.2 = (f32[1,42,1024]{2,0,1:T(1,128)S(1)}, f32[1,42,1024]{2,0,1:T(1,128)}, u32[]{:S(2)}) copy-start(f32[1,42,1024]{2,0,1:T(1,128)} %param.10) | copy-start | bytes 516100
  13.3 298.1 %copy-start.3 = (bf16[1,42,1024]{2,1,0:T(8,128)(2,1)S(1)}, bf16[1,42,1024]{2,1,0:T(8,128)(2,1)}, u32[]{:S(2)}) copy-start(bf16[1,42,1024]{2,1,0:T(8,128)(2,1)} %param.9) | copy-start | bytes 258052
  13.3 542.9 %all-reduce.5.cloned.1.call-start = ((), (), s32[]{:S(2)}) async-start(), calls=%async_computation.2 | async-start | bytes 2752512 | tf_op jit(solution)/shard_map/psum | solution.py:36
  13.4 319.3 %copy-start.4 = (bf16[1,32,512]{2,1,0:T(8,128)(2,1)S(1)}, bf16[1,32,512]{2,1,0:T(8,128)(2,1)}, u32[]{:S(2)}) copy-start(bf16[1,32,512]{2,1,0:T(8,128)(2,1)} %param.11) | copy-start | bytes 98308
  332.7 1.7 copy-start.1
  334.4 308.3 %all-gather.2.cloned.1.call-start = ((), (), s32[]{:S(2)}) async-start(), calls=%async_computation.3 | async-start | bytes 1531904 | tf_op jit(solution)/shard_map/all_gather | solution.py:42
Sparse Core Ops, SparseCore 0:
  13.5 297.8 all-reduce.2
  334.5 221.7 all-reduce.4
  559.9 82.7 all-gather.1
where the time goes:
time: 653 us; the launch traced here: 652 us
  waiting for transfers between devices  605 us (93%)
  blocking collectives  18.6 us (3%)
  between operations  14.6 us (2%)
  matrix products  7.95 us (1%)
    psum x1, waiting for transfers between devices, shards(): lax.psum(jnp.dot(amp_block, weights, preferred_element_type=jnp.float32)...  298 us
    psum x1, waiting for transfers between devices, shards(): lax.psum(partial_cycle.astype(jnp.bfloat16), 'kvir').astype(jnp.float32)  220 us
    all_gather x1, waiting for transfers between devices, shards(): lax.all_gather(local_cycle, 'kvir', axis=1, tiled=True)  86.4 us
    all_to_all x1, blocking collectives, shards(): lax.all_to_all(updated.reshape(rows_dev, tot_count, col_width), 'ktot', s...  18.6 us
  transfers between devices with their start and end apart: 3, of which 3 were waited for; matrix products, arithmetic and copies ran while one was open for 0% of the time, Pallas kernels for 0%

commit v1 on v0

--- a/solution.py
+++ b/solution.py
@@ -2,6 +2,12 @@
 import jax.numpy as jnp
 from jax import lax
 from jax.sharding import PartitionSpec as P
+
+
+def add_all(x, axis):
+    parts = lax.all_gather(x, axis, axis=0, tiled=False)
+    result = parts.sum(axis=0)
+    return result
 
 
 def shards(amplitudes, ladder_integrals, listed, current, denominators, cycle_integrals):
@@ -12,7 +18,7 @@
     width = current.shape[2]
     tot_count = lax.axis_size("ktot")
     vir_count = lax.axis_size("kvir")
-    summed = lax.psum(
+    summed = add_all(
         jnp.dot(amp_block, weights, preferred_element_type=jnp.float32) * scale_mask, "kvir"
     )
     ladder = lax.dynamic_slice_in_dim(summed, lax.axis_index("kvir") * rows_dev, rows_dev, 0)

time: 653 us -> 1310 us (2.01)
  waiting for transfers between devices: 605 us -> 1150 us
  blocking collectives: 18.6 us -> 120 us
  other arithmetic: 1 us -> 18.4 us
    all_gather x0 -> x1, waiting for transfers between devices: none -> 839 us  [add_all(): parts = lax.all_gather(x, axis, axis=0, tiled=False)]
    psum x1 -> x0, waiting for transfers between devices: 298 us -> none  [shards(): lax.psum(jnp.dot(amp_block, weights, preferred_element_type=jnp.float32)...]
    all_to_all x1, blocking collectives: 18.6 us -> 120 us  [shards(): lax.all_to_all(updated.reshape(rows_dev, tot_count, col_width), 'ktot', s...]
    reduce_sum x0 -> x1, other arithmetic: none -> 17.4 us  [add_all(): result = parts.sum(axis=0)]
where the time goes in v1:
time: 1310 us
  waiting for transfers between devices  1150 us (88%)
  blocking collectives  120 us (9%)
  other arithmetic  18.4 us (1%)
  between operations  14.6 us (1%)
    all_gather x1, waiting for transfers between devices, add_all(): parts = lax.all_gather(x, axis, axis=0, tiled=False)  839 us
    psum x1, waiting for transfers between devices, shards(): lax.psum(partial_cycle.astype(jnp.bfloat16), 'kvir').astype(jnp.float32)  219 us
    all_to_all x1, blocking collectives, shards(): lax.all_to_all(updated.reshape(rows_dev, tot_count, col_width), 'ktot', s...  120 us
    all_gather x1, waiting for transfers between devices, shards(): lax.all_gather(local_cycle, 'kvir', axis=1, tiled=True)  86.4 us
  transfers between devices with their start and end apart: 3, of which 3 were waited for; matrix products, arithmetic and copies ran while one was open for 0% of the time, Pallas kernels for 0%

profile of v1, /device:TPU:8, one launch (start us, length us, event | category | flops | bytes accessed | tf_op | source)
XLA Modules:
  0.0 1311.6 jit_solution(13449652044428111938)
XLA Ops:
  7.2 0.0 copy-start
  7.2 0.0 all-gather.6.cloned.1.call-start
  8.0 0.8 copy-done
  8.8 4.5 fusion.3
  13.3 0.0 all-gather.6.cloned.1.call-update
  13.3 0.0 all-reduce.2.cloned.1.call-start
  13.3 838.9 %all-gather.6.cloned.1.call-done = f32[10752,1024]{1,0:T(8,128)} async-done(((f32[672,1024]{1,0:T(8,128)}), f32[10752,1024]{1,0:T(8,128)}) %all-gather.6.cloned.1.call-update) | async-done | bytes 44040208 | tf_op jit(solution)/shard_map/all_gather | solution.py:8
  852.3 17.4 %reduce_sum.9 = f32[672,1024]{1,0:T(8,128)} reduce(f32[16,672,1024]{2,1,0:T(8,128)} %bitcast.33, f32[]{:T(128)} %constant.8.clone.1), dimensions={0}, to_apply=%region_0.0 | reduce | flops 10321920 | bytes 46792708 | tf_op jit(solution)/shard_map/reduce_sum | solution.py:9
  869.7 1.0 fusion.8
  870.7 0.2 copy.15
  870.9 0.4 reshape.17
  871.2 120.1 %all_to_all.5 = bf16[32,2,672]{2,1,0:T(2,128)(2,1)S(1)} all-to-all(bf16[32,2,672]{2,1,0:T(2,128)(2,1)S(1)} %reshape.17), channel_id=1, replica_groups=mesh['ktot'=32,'kvir'=16] {'ktot'}, dimensions={0} | all-to-all | bytes 172032 | tf_op jit(solution)/shard_map/all_to_all | solution.py:27
  991.3 0.4 reshape.18
  991.7 0.4 copy.13
  992.2 0.3 reshape.14
  992.5 1.6 convolution_convert_fusion
  994.1 0.0 all-reduce.2.cloned.1.call-update
  994.1 0.0 all-gather.4.cloned.1.call-start
  994.2 0.7 all-gather.4.cloned.1.call-update
  994.8 1.6 fusion.9
  996.5 219.2 %all-reduce.2.cloned.1.call-done = bf16[1344,512]{1,0:T(8,128)(2,1)} async-done(((bf16[1344,512]{1,0:T(8,128)(2,1)}), bf16[1344,512]{1,0:T(8,128)(2,1)}) %all-reduce.2.cloned.1.call-update) | async-done | bytes 1376272 | tf_op jit(solution)/shard_map/psum | solution.py:42
  1215.6 86.4 %all-gather.4.cloned.1.call-done = bf16[1344,512]{0,1:T(8,128)(2,1)} async-done(((bf16[1344,32]{0,1:T(8,128)(2,1)}), bf16[1344,512]{0,1:T(8,128)(2,1)}) %all-gather.4.cloned.1.call-update) | async-done | bytes 1376272 | tf_op jit(solution)/shard_map/all_gather | solution.py:48
  1302.0 1.8 fusion
  1303.8 1.3 copy.14
  (8 shorter events, 0.0 us)
Async XLA Ops:
  7.2 1.6 copy-start
  7.2 845.1 %all-gather.6.cloned.1.call-start = ((), (), s32[]{:S(2)}) async-start(), calls=%async_computation.3 | async-start | bytes 46792704 | tf_op jit(solution)/shard_map/all_gather | solution.py:8
  13.3 1202.4 %all-reduce.2.cloned.1.call-start = ((), (), s32[]{:S(2)}) async-start(), calls=%async_computation.1 | async-start | bytes 2752512 | tf_op jit(solution)/shard_map/psum | solution.py:42
  852.3 17.4 %copy-start.2 = (f32[1,42,1024]{2,0,1:T(1,128)S(1)}, f32[1,42,1024]{2,0,1:T(1,128)}, u32[]{:S(2)}) copy-start(f32[1,42,1024]{2,0,1:T(1,128)} %param.10) | copy-start | bytes 516100
  852.3 17.4 %copy-start.3 = (bf16[1,42,1024]{2,1,0:T(8,128)(2,1)S(1)}, bf16[1,42,1024]{2,1,0:T(8,128)(2,1)}, u32[]{:S(2)}) copy-start(bf16[1,42,1024]{2,1,0:T(8,128)(2,1)} %param.9) | copy-start | bytes 258052
  869.7 122.8 %copy-start.4 = (bf16[1,32,512]{2,1,0:T(8,128)(2,1)S(1)}, bf16[1,32,512]{2,1,0:T(8,128)(2,1)}, u32[]{:S(2)}) copy-start(bf16[1,32,512]{2,1,0:T(8,128)(2,1)} %param.11) | copy-start | bytes 98308
  992.4 1.7 copy-start.1
  994.1 307.9 %all-gather.4.cloned.1.call-start = ((), (), s32[]{:S(2)}) async-start(), calls=%async_computation.2 | async-start | bytes 1531904 | tf_op jit(solution)/shard_map/all_gather | solution.py:48
Sparse Core Ops, SparseCore 0:
  13.4 838.8 all-gather.5
  994.2 221.3 all-reduce.1
  1219.2 82.7 all-gather.3

commit v2 on v0

--- a/solution.py
+++ b/solution.py
@@ -2,6 +2,11 @@
 import jax.numpy as jnp
 from jax import lax
 from jax.sharding import PartitionSpec as P
+
+
+def gather_over(value, name, d):
+    stack = jnp.stack([value] * lax.axis_size(name))
+    return jnp.concatenate(lax.all_to_all(stack, name, 0, 0), axis=d)
 
 
 def shards(amplitudes, ladder_integrals, listed, current, denominators, cycle_integrals):
@@ -39,7 +44,7 @@
     )
     cycle_out = lax.dot_general(
         cycle_mixed,
-        lax.all_gather(local_cycle, "kvir", axis=1, tiled=True),
+        gather_over(local_cycle, "kvir", 1),
         (((1,), (1,)), ((), ())),
         preferred_element_type=jnp.float32,
     )

time: 653 us -> 624 us (0.956)
  the two profiles are of different devices: /device:TPU:8 before, /device:TPU:16 now
where the time goes in v2:
time: 624 us
  waiting for transfers between devices  563 us (90%)
  blocking collectives  17.7 us (3%)
  between operations  14.9 us (2%)
  starting transfers between devices  12.1 us (2%)
  matrix products  8.3 us (1%)
  local copies, waits for them, and re-layouts  6.52 us (1%)
    psum x1, waiting for transfers between devices, shards(): lax.psum(jnp.dot(amp_block, weights, preferred_element_type=jnp.float32)...  298 us
    psum x1, waiting for transfers between devices, shards(): lax.psum(partial_cycle.astype(jnp.bfloat16), 'kvir').astype(jnp.float32)  265 us
    all_to_all x1, blocking collectives, shards(): lax.all_to_all(updated.reshape(rows_dev, tot_count, col_width), 'ktot', s...  17.7 us
  transfers between devices with their start and end apart: 3, of which 2 were waited for; matrix products, arithmetic and copies ran while one was open for 1% of the time, Pallas kernels for 0%

profile of v2, /device:TPU:16, one launch (start us, length us, event | category | flops | bytes accessed | tf_op | source)
XLA Modules:
  0.0 623.9 jit_solution(5741072749254752000)
XLA Ops:
  7.2 0.0 copy-start
  7.2 0.0 all-reduce.3.cloned.1.call-start
  8.0 0.8 copy-done
  8.8 4.5 fusion.3
  13.3 0.0 all-reduce.3.cloned.1.call-update
  13.3 297.8 %all-reduce.3.cloned.1.call-done = f32[672,1024]{1,0:T(8,128)} async-done(((f32[672,1024]{1,0:T(8,128)}), f32[672,1024]{1,0:T(8,128)}) %all-reduce.3.cloned.1.call-update) | async-done | bytes 2752528 | tf_op jit(solution)/shard_map/psum | solution.py:20
  311.2 1.0 fusion.8
  312.2 0.2 copy.16
  312.4 0.4 reshape.26
  312.7 17.7 %all_to_all.10 = bf16[32,2,672]{2,1,0:T(2,128)(2,1)S(1)} all-to-all(bf16[32,2,672]{2,1,0:T(2,128)(2,1)S(1)} %reshape.26), channel_id=1, replica_groups=mesh['ktot'=32,'kvir'=16] {'ktot'}, dimensions={0} | all-to-all | bytes 172032 | tf_op jit(solution)/shard_map/all_to_all | solution.py:26
  330.4 0.4 reshape.27
  330.8 0.4 copy.14
  331.2 0.3 reshape.22
  331.5 0.0 copy-start.1
  331.5 1.2 stack.3
  332.8 12.1 %all-to-all-start.1 = ((bf16[16,1344,32]{1,2,0:T(8,128)(2,1)}), bf16[16,1344,32]{1,2,0:T(8,128)(2,1)S(1)}, u32[]{:S(2)}, u32[]{:S(2)}) async-start(bf16[16,1344,32]{1,2,0:T(8,128)(2,1)} %stack.3), calls=%async_computation.1 | async-start | bytes 2883584 | tf_op jit(solution)/shard_map/all_to_all | solution.py:9
  344.8 0.0 all-reduce.5.cloned.1.call-start
  344.9 2.5 convolution_convert_fusion
  347.4 0.0 all-reduce.5.cloned.1.call-update
  347.4 1.6 fusion.9
  349.0 265.5 %all-reduce.5.cloned.1.call-done = bf16[1344,512]{1,0:T(8,128)(2,1)} async-done(((bf16[1344,512]{1,0:T(8,128)(2,1)}), bf16[1344,512]{1,0:T(8,128)(2,1)}) %all-reduce.5.cloned.1.call-update) | async-done | bytes 1376272 | tf_op jit(solution)/shard_map/psum | solution.py:41
  614.5 0.0 all-to-all-done.1
  614.5 1.3 fusion
  615.8 1.3 copy.15
  (5 shorter events, 0.0 us)
Async XLA Ops:
  7.2 1.6 copy-start
  7.2 304.0 %all-reduce.3.cloned.1.call-start = ((), (), s32[]{:S(2)}) async-start(), calls=%async_computation.2 | async-start | bytes 5505024 | tf_op jit(solution)/shard_map/psum | solution.py:20
  13.3 297.9 %copy-start.2 = (f32[1,42,1024]{2,0,1:T(1,128)S(1)}, f32[1,42,1024]{2,0,1:T(1,128)}, u32[]{:S(2)}) copy-start(f32[1,42,1024]{2,0,1:T(1,128)} %param.10) | copy-start | bytes 516100
  13.3 297.9 %copy-start.3 = (bf16[1,42,1024]{2,1,0:T(8,128)(2,1)S(1)}, bf16[1,42,1024]{2,1,0:T(8,128)(2,1)}, u32[]{:S(2)}) copy-start(bf16[1,42,1024]{2,1,0:T(8,128)(2,1)} %param.9) | copy-start | bytes 258052
  331.5 1.2 copy-start.1
  332.8 281.7 %all-to-all-start.1 = ((bf16[16,1344,32]{1,2,0:T(8,128)(2,1)}), bf16[16,1344,32]{1,2,0:T(8,128)(2,1)S(1)}, u32[]{:S(2)}, u32[]{:S(2)}) async-start(bf16[16,1344,32]{1,2,0:T(8,128)(2,1)} %stack.3), calls=%async_computation.1 | async-start | bytes 2883584 | tf_op jit(solution)/shard_map/all_to_all | solution.py:9
  344.8 269.7 %all-reduce.5.cloned.1.call-start = ((), (), s32[]{:S(2)}) async-start(), calls=%async_computation.3 | async-start | bytes 2752512 | tf_op jit(solution)/shard_map/psum | solution.py:41
Sparse Core Ops, SparseCore 0:
  13.4 297.6 all-reduce.2
  348.6 265.8 all-reduce.4
